TPU v7x, 128 devices: a whole 4x4x4 slice. The times are simulated.
128 devices in a mesh: tm: 16 (over y, x), tile: 8 (over z, core).
Axes of the slice: x: 4, y: 4, z: 4, core: 2. Of those that a mesh axis runs over, the one named last changes fastest.
Arguments:
- queries: bfloat16 [16384, 1536], P(('tm', 'tile')), may hold values from -16 to 16
- keys: bfloat16 [16384, 1536], P(('tm', 'tile')), may hold values from -16 to 16
- values: bfloat16 [16384, 1536], P(('tm', 'tile')), may hold values from -6 to 6
- grad_out: bfloat16 [16384, 1536], P(('tm', 'tile')), may hold values from -6 to 6
- span_of_group: int32 [16], replicated, may hold values from 0 to 15, each once
- noise_level: int32 [16], replicated, may hold values from 0 to 999
- next_live: int32 [128], replicated, may hold values 0 or 1
- level_bias: float32 [1000, 12], replicated, may hold values from -2 to 2
Outputs:
- attended: bfloat16 [16384, 1536], P(('tm', 'tile'))
- grad_queries: bfloat16 [16384, 1536], P(('tm', 'tile'))
- grad_keys: bfloat16 [16384, 1536], P(('tm', 'tile'))
- grad_values: bfloat16 [16384, 1536], P(('tm', 'tile'))
Inputs may be any that keep to these rules, and one draw needn't show every extreme that they name: span_of_group is a permutation of 0 to 15.
All inputs are finite; a program needn't handle non-finite values.
Results may differ from a plain program's by a relative error of at most 0.019.
Values may be sent and summed in bfloat16 or wider, within the bound.
A program may use at most 256 MiB of HBM per device.

v0:
```python
import math

import jax
import jax.numpy as jnp
from jax import lax
from jax.sharding import PartitionSpec as P


def shifted(value, axis, by):
    count = lax.axis_size(axis)
    return lax.ppermute(value, axis, [(i, (i + by) % count) for i in range(count)])


def pick_entry(table, index):
    spots = jnp.arange(table.shape[0], dtype=jnp.int32)
    return jnp.sum(jnp.where(spots == index, table, 0), axis=0)


def per_device(queries, keys, values, grad_out, span_of_group, noise_level, next_live, level_bias):
    tok_rows, model_width = queries.shape
    head_count = level_bias.shape[1]
    head_width = model_width // head_count
    inv_root = 1.0 / math.sqrt(head_width)
    groups = lax.axis_size("tm")
    tile_count = lax.axis_size("tile")
    my_group = lax.axis_index("tm")
    my_tile = lax.axis_index("tile")
    group_ids = jnp.arange(groups, dtype=jnp.int32)
    own_span = pick_entry(span_of_group, my_group)
    level_of = jnp.sum(
        jnp.where(span_of_group[:, None] == group_ids[None, :], noise_level[None, :], 0), axis=1
    )
    level_ids = jnp.arange(level_bias.shape[0], dtype=jnp.int32)
    level_table = (level_of[:, None] == level_ids[None, :]).astype(jnp.float32)
    group_bias = jnp.dot(
        level_table, level_bias, precision=lax.Precision.HIGHEST, preferred_element_type=jnp.float32
    )
    second_half = jnp.arange(2 * tok_rows, dtype=jnp.int32) >= tok_rows
    first_half = jnp.logical_not(second_half)
    live_table = next_live.reshape(groups, tile_count)
    live_here = pick_entry(next_live, my_group * tile_count + my_tile)
    attend = span_of_group <= own_span
    key_mask = attend[:, None] & (first_half[None, :] | (live_here == 1))
    near_k, near_v = shifted((keys, values), "tile", -1)
    past_k, past_v, ahead_k, ahead_v = (
        lax.all_gather(keys[None], "tm", axis=0, tiled=True),
        lax.all_gather(values[None], "tm", axis=0, tiled=True),
        lax.all_gather(near_k[None], "tm", axis=0, tiled=True),
        lax.all_gather(near_v[None], "tm", axis=0, tiled=True),
    )
    all_keys = jnp.concatenate([past_k, ahead_k], axis=1).reshape(
        groups, 2 * tok_rows, head_count, head_width
    )
    all_values = jnp.concatenate([past_v, ahead_v], axis=1).reshape(
        groups, 2 * tok_rows, head_count, head_width
    )
    query_heads = queries.reshape(tok_rows, head_count, head_width)
    grad_heads = grad_out.reshape(tok_rows, head_count, head_width)
    scores = jnp.einsum("qhe,jkhe->jhqk", query_heads, all_keys, preferred_element_type=jnp.float32)
    scores = scores * inv_root + group_bias[:, :, None, None]
    scores = jnp.where(key_mask[:, None, None, :], scores, -1e30)
    row_peak = jnp.max(scores, axis=(0, 3))
    log_total = row_peak + jnp.log(
        jnp.sum(jnp.exp(scores - row_peak[None, :, :, None]), axis=(0, 3))
    )
    weights_full = jnp.exp(scores - log_total[None, :, :, None])
    weights_low = weights_full.astype(jnp.bfloat16)
    attended = jnp.einsum(
        "jhqk,jkhe->qhe", weights_low, all_values, preferred_element_type=jnp.float32
    ).astype(jnp.bfloat16)
    row_delta = jnp.sum(grad_heads.astype(jnp.float32) * attended.astype(jnp.float32), axis=2).T
    grad_weights = jnp.einsum(
        "qhe,jkhe->jhqk", grad_heads, all_values, preferred_element_type=jnp.float32
    )
    grad_scores = (weights_full * (grad_weights - row_delta[None, :, :, None]) * inv_root).astype(
        jnp.bfloat16
    )
    grad_queries = jnp.einsum(
        "jhqk,jkhe->qhe", grad_scores, all_keys, preferred_element_type=jnp.float32
    )
    grad_queries = grad_queries.astype(jnp.bfloat16).reshape(tok_rows, model_width)
    near_q, near_g = shifted((queries, grad_out), "tile", 1)
    near_lse, near_delta = shifted((log_total, row_delta), "tile", 1)
    past_q, past_g, prev_q, prev_g = (
        lax.all_gather(queries[None], "tm", axis=0, tiled=True),
        lax.all_gather(grad_out[None], "tm", axis=0, tiled=True),
        lax.all_gather(near_q[None], "tm", axis=0, tiled=True),
        lax.all_gather(near_g[None], "tm", axis=0, tiled=True),
    )
    past_lse, past_delta, prev_lse, prev_delta = (
        lax.all_gather(log_total[None], "tm", axis=0, tiled=True),
        lax.all_gather(row_delta[None], "tm", axis=0, tiled=True),
        lax.all_gather(near_lse[None], "tm", axis=0, tiled=True),
        lax.all_gather(near_delta[None], "tm", axis=0, tiled=True),
    )
    source_q = jnp.concatenate([past_q, prev_q], axis=1).reshape(
        groups, 2 * tok_rows, head_count, head_width
    )
    source_g = jnp.concatenate([past_g, prev_g], axis=1).reshape(
        groups, 2 * tok_rows, head_count, head_width
    )
    source_lse = jnp.concatenate([past_lse, prev_lse], axis=2)
    source_delta = jnp.concatenate([past_delta, prev_delta], axis=2)
    prev_tile = (my_tile + tile_count - 1) % tile_count
    tile_ids = jnp.arange(tile_count, dtype=jnp.int32)
    prev_live = jnp.sum(jnp.where(tile_ids[None, :] == prev_tile, live_table, 0), axis=1)
    seen_by = own_span <= span_of_group
    query_mask = seen_by[:, None] & (first_half[None, :] | (prev_live[:, None] == 1))
    my_bias = jnp.sum(jnp.where(group_ids[:, None] == my_group, group_bias, 0.0), axis=0)
    key_heads = keys.reshape(tok_rows, head_count, head_width)
    value_heads = values.reshape(tok_rows, head_count, head_width)
    back_scores = jnp.einsum(
        "gqhe,khe->ghqk", source_q, key_heads, preferred_element_type=jnp.float32
    )
    back_scores = back_scores * inv_root + my_bias[None, :, None, None]
    back_full = jnp.where(
        query_mask[:, None, :, None], jnp.exp(back_scores - source_lse[:, :, :, None]), 0.0
    )
    back_low = back_full.astype(jnp.bfloat16)
    back_grad = jnp.einsum(
        "gqhe,khe->ghqk", source_g, value_heads, preferred_element_type=jnp.float32
    )
    back_ds = (back_full * (back_grad - source_delta[:, :, :, None]) * inv_root).astype(
        jnp.bfloat16
    )
    grad_keys = jnp.einsum("ghqk,gqhe->khe", back_ds, source_q, preferred_element_type=jnp.float32)
    grad_values = jnp.einsum(
        "ghqk,gqhe->khe", back_low, source_g, preferred_element_type=jnp.float32
    )
    grad_keys = grad_keys.astype(jnp.bfloat16).reshape(tok_rows, model_width)
    grad_values = grad_values.astype(jnp.bfloat16).reshape(tok_rows, model_width)
    return (attended.reshape(tok_rows, model_width), grad_queries, grad_keys, grad_values)


def solution(mesh):
    in_specs = (
        P(("tm", "tile"), None),
        P(("tm", "tile"), None),
        P(("tm", "tile"), None),
        P(("tm", "tile"), None),
        P(),
        P(),
        P(),
        P(),
    )
    out_specs = (
        P(("tm", "tile"), None),
        P(("tm", "tile"), None),
        P(("tm", "tile"), None),
        P(("tm", "tile"), None),
    )
    return jax.shard_map(
        per_device, mesh=mesh, in_specs=in_specs, out_specs=out_specs, check_vma=False
    )
```

profile of v0, /device:TPU:0, one launch (start us, length us, event | category | flops | bytes accessed | tf_op | source)
XLA Modules:
  0.0 683.0 jit_solution(12979468806883609917)
XLA Ops:
  52.0 21.8 %all-gather.25.cloned.1.call-done = bf16[2048,1536]{1,0:T(8,128)(2,1)} async-done(((bf16[128,1536]{1,0:T(8,128)(2,1)}), bf16[2048,1536]{1,0:T(8,128)(2,1)}) %all-gather.25.cloned.1.call-update) | async-done | bytes 6291472 | tf_op jit(solution)/shard_map/all_gather | solution.py:47
  73.8 63.6 %all-gather.27.cloned.1.call-done = bf16[2048,1536]{1,0:T(8,128)(2,1)} async-done(((bf16[128,1536]{1,0:T(8,128)(2,1)}), bf16[2048,1536]{1,0:T(8,128)(2,1)}) %all-gather.27.cloned.1.call-update) | async-done | bytes 6291472 | tf_op jit(solution)/shard_map/all_gather | solution.py:49
  147.9 16.7 %copy.101 = bf16[16,256,1536]{1,2,0:T(8,128)(2,1)} copy(bf16[16,256,1536]{2,1,0:T(8,128)(2,1)} %pad_maximum_fusion) | data formatting | bytes 25165824 | tf_op jit(solution)/shard_map/concatenate | solution.py:54
  164.6 35.8 %all-gather.29.cloned.1.call-done = bf16[2048,1536]{1,0:T(8,128)(2,1)} async-done(((bf16[128,1536]{1,0:T(8,128)(2,1)}), bf16[2048,1536]{1,0:T(8,128)(2,1)}) %all-gather.29.cloned.1.call-update) | async-done | bytes 6291472 | tf_op jit(solution)/shard_map/all_gather | solution.py:46
  200.4 63.5 %all-gather.31.cloned.1.call-done = bf16[2048,1536]{1,0:T(8,128)(2,1)} async-done(((bf16[128,1536]{1,0:T(8,128)(2,1)}), bf16[2048,1536]{1,0:T(8,128)(2,1)}) %all-gather.31.cloned.1.call-update) | async-done | bytes 6291472 | tf_op jit(solution)/shard_map/all_gather | solution.py:48
  274.3 16.7 %copy.102 = bf16[16,256,1536]{1,2,0:T(8,128)(2,1)} copy(bf16[16,256,1536]{2,1,0:T(8,128)(2,1)} %pad_maximum_fusion.1) | data formatting | bytes 25165824 | tf_op jit(solution)/shard_map/concatenate | solution.py:51
  291.1 15.8 %fusion.26 = (f32[12,128]{1,0:T(8,128)S(1)}, f32[12,16,256,128]{3,2,1,0:T(8,128)}) fusion(f32[16,12]{0,1:T(8,128)S(1)} %copy.106, pred[16,256]{1,0:T(8,128)(4,1)S(1)} %broadcast_and_fusion, bf16[128,12,128,1]{0,2,3,1:T(8,128)(2,1)S(1)} %bitcast.134, bf16[16,256,12,128]{1,3,2,0:T(8,128)(2,1)} %bitcast.118), kind=kOutput, calls=%fused_computation.36 | convolution fusion | flops 1635777024 | bytes 38152960 | tf_op jit(solution)/shard_map/qhe,jkhe->jhqk/dot_general | solution.py:59
  306.9 12.4 %exponential_reduce_fusion = f32[12,128]{1,0:T(8,128)S(1)} fusion(f32[12,128]{1,0:T(8,128)S(1)} %get-tuple-element.28, f32[16,12]{0,1:T(8,128)S(1)} %copy.106, f32[12,16,256,128]{3,2,1,0:T(8,128)} %get-tuple-element.29, pred[16,256]{1,0:T(8,128)(4,1)S(1)} %broadcast_and_fusion), kind=kLoop, calls=%fused_computation.13 | loop fusion | flops 31455744 | bytes 25182976 | tf_op jit(solution)/shard_map/reduce_sum | solution.py:64
  319.3 16.1 %multiply_reduce_fusion = (f32[128,12]{0,1:T(8,128)S(1)}, bf16[12,128,128]{2,1,0:T(8,128)(2,1)S(1)}) fusion(bf16[128,12,128]{0,2,1:T(8,128)(2,1)S(1)} %bitcast.132, bf16[16,256,12,128]{1,3,2,0:T(8,128)(2,1)} %bitcast.116, f32[12,128]{1,0:T(8,128)S(1)} %log_add_fusion, f32[16,12]{0,1:T(8,128)S(1)} %copy.106, f32[12,16,256,128]{3,2,1,0:T(8,128)} %get-tuple-element.29, ...), kind=kOutput, calls=%fused_computation.45 | convolution fusion | flops 1643051520 | bytes 38552320 | tf_op jit(solution)/shard_map/jhqk,jkhe->qhe/dot_general | solution.py:68
  337.0 53.2 %all-gather.39.cloned.1.call-done = bf16[2048,1536]{1,0:T(8,128)(2,1)} async-done(((bf16[128,1536]{1,0:T(8,128)(2,1)}), bf16[2048,1536]{1,0:T(8,128)(2,1)}) %all-gather.39.cloned.1.call-update) | async-done | bytes 6291472 | tf_op jit(solution)/shard_map/all_gather | solution.py:88
  390.2 10.5 %pad_maximum_fusion.3 = bf16[16,256,1536]{2,1,0:T(8,128)(2,1)} fusion(bf16[16,128,1536]{2,1,0:T(8,128)(2,1)} %bitcast.127, bf16[16,128,1536]{2,1,0:T(8,128)(2,1)} %bitcast.123), kind=kLoop, calls=%fused_computation.19 | loop fusion | flops 25165824 | bytes 25165824 | tf_op jit(solution)/shard_map/concatenate | solution.py:99
  400.7 15.9 %copy.117 = bf16[16,256,1536]{1,2,0:T(8,128)(2,1)} copy(bf16[16,256,1536]{2,1,0:T(8,128)(2,1)} %pad_maximum_fusion.3) | data formatting | bytes 25165824 | tf_op jit(solution)/shard_map/concatenate | solution.py:99
  416.5 24.4 %all-gather.12 = f32[16,12,128]{2,1,0:T(8,128)S(1)} all-gather(f32[1,12,128]{2,1,0:T(8,128)S(1)} %bitcast.139), channel_id=8, replica_groups=mesh['tm'=16,'tile'=8] {'tm'}, dimensions={0}, use_global_device_ids=true | all-gather | bytes 104448 | tf_op jit(solution)/shard_map/all_gather | solution.py:91
  440.9 21.8 %fusion.6 = bf16[16,12,128,256]{2,3,0,1:T(8,128)(2,1)} fusion(f32[12,128]{1,0:T(8,128)S(1)} %bitcast.142, f32[12,128]{1,0:T(8,128)S(1)} %log_add_fusion, f32[16,12]{0,1:T(8,128)S(1)} %copy.106, f32[12,16,256,128]{3,2,1,0:T(8,128)} %get-tuple-element.29, pred[16,256]{1,0:T(8,128)(4,1)S(1)} %broadcast_and_fusion, bf16[128,12,128,1]{0,2,3,1:T(8,128)(2,1)S(1)} %bitcast.133, ...), kind=kOutput, calls=%fused_computation.9 | convolution fusion | flops 1660944384 | bytes 50742016 | tf_op jit(solution)/shard_map/qhe,jkhe->jhqk/dot_general | solution.py:72
  462.7 12.0 %fusion.39 = bf16[12,128,128]{2,1,0:T(8,128)(2,1)S(1)} fusion(bf16[16,256,12,128]{1,3,2,0:T(8,128)(2,1)} %bitcast.119, bf16[16,12,128,256]{2,3,0,1:T(8,128)(2,1)} %fusion.6), kind=kOutput, calls=%fused_computation.41 | convolution fusion | flops 1610809344 | bytes 25559040 | tf_op jit(solution)/shard_map/jhqk,jkhe->qhe/dot_general | solution.py:78
  474.7 42.6 %all-gather.35.cloned.1.call-done = bf16[2048,1536]{1,0:T(8,128)(2,1)} async-done(((bf16[128,1536]{1,0:T(8,128)(2,1)}), bf16[2048,1536]{1,0:T(8,128)(2,1)}) %all-gather.35.cloned.1.call-update) | async-done | bytes 6291472 | tf_op jit(solution)/shard_map/all_gather | solution.py:87
  527.8 13.1 %fusion.10 = f32[12,16,256,128]{3,2,1,0:T(8,128)} fusion(bf16[128,12,128,1]{0,2,3,1:T(8,128)(2,1)S(1)} %bitcast.130, bf16[16,256,12,128]{1,3,2,0:T(8,128)(2,1)} %bitcast.114), kind=kOutput, calls=%fused_computation.20 | convolution fusion | flops 1610612736 | bytes 38141952 | tf_op jit(solution)/shard_map/gqhe,khe->ghqk/dot_general | solution.py:120
  540.9 23.3 %all-gather.14 = f32[16,12,128]{2,1,0:T(8,128)S(1)} all-gather(f32[1,12,128]{2,1,0:T(8,128)S(1)} %bitcast.143), channel_id=12, replica_groups=mesh['tm'=16,'tile'=8] {'tm'}, dimensions={0}, use_global_device_ids=true | all-gather | bytes 104448 | tf_op jit(solution)/shard_map/all_gather | solution.py:92
  566.1 16.6 %copy.112 = bf16[16,256,1536]{1,2,0:T(8,128)(2,1)} copy(bf16[16,256,1536]{2,1,0:T(8,128)(2,1)} %pad_maximum_fusion.2) | data formatting | bytes 25165824 | tf_op jit(solution)/shard_map/concatenate | solution.py:96
  582.7 21.5 %all-gather.13 = f32[16,12,128]{2,1,0:T(8,128)S(1)} all-gather(f32[1,12,128]{2,1,0:T(8,128)S(1)} %bitcast.144), channel_id=9, replica_groups=mesh['tm'=16,'tile'=8] {'tm'}, dimensions={0}, use_global_device_ids=true | all-gather | bytes 104448 | tf_op jit(solution)/shard_map/all_gather | solution.py:93
  604.4 23.3 %all-gather.15 = f32[16,12,128]{2,1,0:T(8,128)S(1)} all-gather(f32[1,12,128]{2,1,0:T(8,128)S(1)} %bitcast.140), channel_id=13, replica_groups=mesh['tm'=16,'tile'=8] {'tm'}, dimensions={0}, use_global_device_ids=true | all-gather | bytes 104448 | tf_op jit(solution)/shard_map/all_gather | solution.py:94
  627.8 23.3 %fusion.9 = (bf16[16,12,256,128]{3,2,0,1:T(8,128)(2,1)}, bf16[16,12,256,128]{3,2,0,1:T(8,128)(2,1)}) fusion(f32[16,12,256]{2,0,1:T(8,128)S(1)} %copy.116, f32[12]{0:T(128)S(1)} %get-tuple-element.32, pred[16,256]{1,0:T(8,128)(4,1)S(1)} %or_and_fusion, f32[16,12,256]{2,0,1:T(8,128)S(1)} %copy.121, f32[12,16,256,128]{3,2,1,0:T(8,128)} %fusion.10, ...), kind=kOutput, calls=%fused_computation.15 | convolution fusion | flops 1667235840 | bytes 63705136 | tf_op jit(solution)/shard_map/gqhe,khe->ghqk/dot_general | solution.py:112
  651.1 11.6 %fusion.48 = bf16[12,128,128]{2,1,0:T(8,128)(2,1)S(1)} fusion(bf16[16,256,12,128]{1,3,2,0:T(8,128)(2,1)} %bitcast.121, bf16[16,12,256,128]{3,2,0,1:T(8,128)(2,1)} %get-tuple-element.25), kind=kOutput, calls=%fused_computation.44 | convolution fusion | flops 1610809344 | bytes 25559040 | tf_op jit(solution)/shard_map/ghqk,gqhe->khe/dot_general | solution.py:126
  663.6 11.6 %fusion.45 = bf16[12,128,128]{2,1,0:T(8,128)(2,1)S(1)} fusion(bf16[16,256,12,128]{1,3,2,0:T(8,128)(2,1)} %bitcast.115, bf16[16,12,256,128]{3,2,0,1:T(8,128)(2,1)} %get-tuple-element.24), kind=kOutput, calls=%fused_computation.43 | convolution fusion | flops 1610809344 | bytes 25559040 | tf_op jit(solution)/shard_map/ghqk,gqhe->khe/dot_general | solution.py:127
  (73 shorter events, 81.0 us)
Async XLA Ops:
  7.2 38.1 %copy-start = (f32[1000,12]{0,1:T(8,128)S(1)}, f32[1000,12]{0,1:T(8,128)}, u32[]{:S(2)}) copy-start(f32[1000,12]{0,1:T(8,128)} %param.15) | copy-start | bytes 144004
  7.2 66.6 %all-gather.25.cloned.1.call-start = ((), (), s32[]{:S(2)}) async-start(), calls=%async_computation | async-start | bytes 6684672 | tf_op jit(solution)/shard_map/all_gather | solution.py:47
  7.9 129.5 %all-gather.27.cloned.1.call-start = ((), (), s32[]{:S(2)}) async-start(), calls=%async_computation.1 | async-start | bytes 6684672 | tf_op jit(solution)/shard_map/all_gather | solution.py:49
  8.0 9.2 %collective-permute-start = (bf16[128,1536]{1,0:T(8,128)(2,1)}, bf16[128,1536]{1,0:T(8,128)(2,1)S(1)}, u32[]{:S(2)}, u32[]{:S(2)}) collective-permute-start(bf16[128,1536]{1,0:T(8,128)(2,1)} %param.10), channel_id=1, source_target_pairs={{0,7},{1,0},{2,1},{3,2},{4,3},{5,4},{6,5},{7,6},{8,15},{9,8},{10,9... | collective-permute-start | bytes 1179656 | tf_op jit(solution)/shard_map/ppermute | solution.py:11
  17.2 0.7 copy-start.2
  17.9 182.5 %all-gather.29.cloned.1.call-start = ((), (), s32[]{:S(2)}) async-start(), calls=%async_computation.2 | async-start | bytes 6684672 | tf_op jit(solution)/shard_map/all_gather | solution.py:46
  18.7 245.2 %all-gather.31.cloned.1.call-start = ((), (), s32[]{:S(2)}) async-start(), calls=%async_computation.3 | async-start | bytes 6684672 | tf_op jit(solution)/shard_map/all_gather | solution.py:48
  18.7 8.6 %collective-permute-start.1 = (bf16[128,1536]{1,0:T(8,128)(2,1)}, bf16[128,1536]{1,0:T(8,128)(2,1)S(1)}, u32[]{:S(2)}, u32[]{:S(2)}) collective-permute-start(bf16[128,1536]{1,0:T(8,128)(2,1)} %param.9), channel_id=1, source_target_pairs={{0,7},{1,0},{2,1},{3,2},{4,3},{5,4},{6,5},{7,6},{8,15},{9,8},{10,9... | collective-permute-start | bytes 1179656 | tf_op jit(solution)/shard_map/ppermute | solution.py:11
  27.4 0.7 copy-start.5
  28.1 308.9 %all-gather.37.cloned.1.call-start = ((), (), s32[]{:S(2)}) async-start(), calls=%async_computation.6 | async-start | bytes 6684672 | tf_op jit(solution)/shard_map/all_gather | solution.py:86
  28.7 361.5 %all-gather.39.cloned.1.call-start = ((), (), s32[]{:S(2)}) async-start(), calls=%async_computation.7 | async-start | bytes 6684672 | tf_op jit(solution)/shard_map/all_gather | solution.py:88
  28.8 9.1 %collective-permute-start.4 = (bf16[128,1536]{1,0:T(8,128)(2,1)}, bf16[128,1536]{1,0:T(8,128)(2,1)S(1)}, u32[]{:S(2)}, u32[]{:S(2)}) collective-permute-start(bf16[128,1536]{1,0:T(8,128)(2,1)} %param.11), channel_id=1, source_target_pairs={{0,1},{1,2},{2,3},{3,4},{4,5},{5,6},{6,7},{7,0},{8,9},{9,10},{10,1... | collective-permute-start | bytes 1179656 | tf_op jit(solution)/shard_map/ppermute | solution.py:11
  37.9 0.7 copy-start.3
  38.6 436.1 %all-gather.33.cloned.1.call-start = ((), (), s32[]{:S(2)}) async-start(), calls=%async_computation.4 | async-start | bytes 6684672 | tf_op jit(solution)/shard_map/all_gather | solution.py:85
  39.4 478.0 %all-gather.35.cloned.1.call-start = ((), (), s32[]{:S(2)}) async-start(), calls=%async_computation.5 | async-start | bytes 6684672 | tf_op jit(solution)/shard_map/all_gather | solution.py:87
  39.4 11.8 %collective-permute-start.2 = (bf16[128,1536]{1,0:T(8,128)(2,1)}, bf16[128,1536]{1,0:T(8,128)(2,1)S(1)}, u32[]{:S(2)}, u32[]{:S(2)}) collective-permute-start(bf16[128,1536]{1,0:T(8,128)(2,1)} %param.8), channel_id=1, source_target_pairs={{0,1},{1,2},{2,3},{3,4},{4,5},{5,6},{6,7},{7,0},{8,9},{9,10},{10,1... | collective-permute-start | bytes 1179656 | tf_op jit(solution)/shard_map/ppermute | solution.py:11
  51.2 0.7 copy-start.4
  319.3 263.5 %collective-permute-start.3 = (f32[12,128]{1,0:T(8,128)S(1)}, f32[12,128]{1,0:T(8,128)S(1)}, u32[]{:S(2)}, u32[]{:S(2)}) collective-permute-start(f32[12,128]{1,0:T(8,128)S(1)} %log_add_fusion), channel_id=1, source_target_pairs={{0,1},{1,2},{2,3},{3,4},{4,5},{5,6},{6,7},{7,0},{8,9},{9,10},{10,1... | collective-permute-start | bytes 18440 | tf_op jit(solution)/shard_map/ppermute | solution.py:11
  335.4 269.0 %collective-permute-start.5 = (f32[12,128]{1,0:T(8,128)S(1)}, f32[12,128]{1,0:T(8,128)S(1)}, u32[]{:S(2)}, u32[]{:S(2)}) collective-permute-start(f32[12,128]{1,0:T(8,128)S(1)} %bitcast.141), channel_id=1, source_target_pairs={{0,1},{1,2},{2,3},{3,4},{4,5},{5,6},{6,7},{7,0},{8,9},{9,10},{10,1... | collective-permute-start | bytes 18440 | tf_op jit(solution)/shard_map/ppermute | solution.py:11
  663.6 12.6 %copy-start.1 = (f32[1000,12]{0,1:T(8,128)S(1)}, f32[1000,12]{0,1:T(8,128)}, u32[]{:S(2)}) copy-start(f32[1000,12]{0,1:T(8,128)} %param.15) | copy-start | bytes 144004
Sparse Core Ops, SparseCore 0:
  10.1 63.6 all-gather.24
  76.5 60.8 all-gather.26
  139.5 60.8 all-gather.28
  203.0 60.8 all-gather.30
  265.8 60.8 all-gather.36
  329.3 60.8 all-gather.38
  392.3 61.3 all-gather.32
  456.5 60.8 all-gather.34
where the time goes:
time: 685 us; the launch traced here: 683 us
  waiting for transfers between devices  303 us (44%)
  matrix products  125 us (18%)
  blocking collectives  92.5 us (14%)
  local copies, waits for them, and re-layouts  78.6 us (11%)
  other arithmetic  59.4 us (9%)
  between operations  15 us (2%)
  starting transfers between devices  8.61 us (1%)
    all_gather x1, waiting for transfers between devices, per_device(): lax.all_gather(near_v[None], 'tm', axis=0, tiled=True)  63.6 us
    all_gather x1, waiting for transfers between devices, per_device(): lax.all_gather(near_k[None], 'tm', axis=0, tiled=True)  63.5 us
    all_gather x1, waiting for transfers between devices, per_device(): lax.all_gather(near_g[None], 'tm', axis=0, tiled=True)  53.2 us
    all_gather x1, waiting for transfers between devices, per_device(): lax.all_gather(near_q[None], 'tm', axis=0, tiled=True)  42.6 us
    all_gather x1, waiting for transfers between devices, per_device(): lax.all_gather(keys[None], 'tm', axis=0, tiled=True)  35.8 us
    all_gather x1, blocking collectives, per_device(): lax.all_gather(log_total[None], 'tm', axis=0, tiled=True)  24.4 us
    all_gather x1, blocking collectives, per_device(): lax.all_gather(row_delta[None], 'tm', axis=0, tiled=True)  23.3 us
    all_gather x1, blocking collectives, per_device(): lax.all_gather(near_delta[None], 'tm', axis=0, tiled=True)  23.3 us
  transfers between devices with their start and end apart: 14, of which 9 were waited for; matrix products, arithmetic and copies ran while one was open for 31% of the time, Pallas kernels for 0%

commit v1 on v0

v1 whole, which is shorter than its diff:
```python
import functools
import math

import jax
import jax.numpy as jnp
from jax import lax
from jax.experimental import pallas as pl
from jax.experimental.pallas import tpu as pltpu
from jax.sharding import PartitionSpec as P

SIDE = 4
GROUPS = 16
TILES = 8
HEADS = 12
ROWS = 128
WIDTH = 128
PAIR = 2 * ROWS
PAIRS = GROUPS // 2
NEG = -1e30
LOG2E = math.log2(math.e)
MESH = pl.DeviceIdType.MESH
OFFSETS = [(dy, dx) for dy in range(SIDE) for dx in range(SIDE) if (dy, dx) != (0, 0)]
ORDER = sorted(OFFSETS, key=lambda o: -(min(o[0], SIDE - o[0]) + min(o[1], SIDE - o[1])))


def head_of(y, x):
    skipped = SIDE - 1 - y
    return 3 * y + x - (x > skipped).astype(jnp.int32), x != skipped


def place():
    me = lax.axis_index("tm")
    tile = lax.axis_index("tile")
    return me, tile, lax.div(me, SIDE), lax.rem(me, SIDE)


def partner(y, x, dy, dx):
    py = lax.rem(y + dy, SIDE)
    px = lax.rem(x + dx, SIDE)
    head, live = head_of(py, px)
    return py * SIDE + px, head, live


def columns(head):
    return pl.ds(pl.multiple_of(head * WIDTH, WIDTH), WIDTH)


def meet(me, tile, y, x, before, after):
    barrier = pltpu.get_barrier_semaphore()
    for dy, dx in OFFSETS:
        other, _, _ = partner(y, x, dy, dx)
        pl.semaphore_signal(barrier, inc=1, device_id=(other, tile), device_id_type=MESH)
    for other in (before, after):
        pl.semaphore_signal(barrier, inc=1, device_id=(me, other), device_id_type=MESH)
    pl.semaphore_wait(barrier, len(OFFSETS) + 2)


def await_bytes(ref, sem):
    pltpu.make_async_copy(ref, ref, sem).wait()


def send(src, dst, send_sem, recv_sem, device):
    pltpu.make_async_remote_copy(
        src_ref=src, dst_ref=dst, send_sem=send_sem, recv_sem=recv_sem,
        device_id=device, device_id_type=MESH,
    ).start()


def spread_kernel(q_ref, k_ref, v_ref, g_ref, held, out_sem, kv_sem, qg_sem, near_out, near_in):
    me, tile, y, x = place()
    before = lax.rem(tile + TILES - 1, TILES)
    after = lax.rem(tile + 1, TILES)
    my_head, active = head_of(y, x)
    meet(me, tile, y, x, before, after)
    own = columns(my_head)

    @pl.when(active)
    def _():
        pltpu.make_async_copy(k_ref.at[:, own], held.at[2, me], kv_sem.at[me]).start()
        pltpu.make_async_copy(v_ref.at[:, own], held.at[3, me], kv_sem.at[me]).start()
        pltpu.make_async_copy(q_ref.at[:, own], held.at[0, me], qg_sem.at[me]).start()
        pltpu.make_async_copy(g_ref.at[:, own], held.at[1, me], qg_sem.at[me]).start()

    def give(pairs, recv_sem):
        for n, (dy, dx) in enumerate(ORDER):
            other, head, live = partner(y, x, dy, dx)

            @pl.when(live)
            def _(n=n, other=other, head=head):
                for ref, slot in pairs:
                    send(ref.at[:, columns(head)], held.at[slot, me], out_sem.at[n],
                         recv_sem.at[me], (other, tile))

    give([(k_ref, 2), (v_ref, 3)], kv_sem)
    give([(q_ref, 0), (g_ref, 1)], qg_sem)

    @pl.when(active)
    def _():
        sources = [partner(y, x, SIDE - dy, SIDE - dx)[0] for dy, dx in ORDER]
        for g in [me] + sources:
            await_bytes(held.at[pl.ds(2, 2), g], kv_sem.at[g])
            send(held.at[pl.ds(2, 2), g], held.at[pl.ds(4, 2), g], near_out.at[g],
                 near_in.at[g], (me, before))
        for g in [me] + sources:
            await_bytes(held.at[pl.ds(0, 2), g], qg_sem.at[g])
            await_bytes(held.at[pl.ds(2, 2), g], near_out.at[g])
            await_bytes(held.at[pl.ds(4, 2), g], near_in.at[g])

    for n, (dy, dx) in enumerate(ORDER):
        _, _, live = partner(y, x, dy, dx)

        @pl.when(live)
        def _(n=n):
            await_bytes(held.at[pl.ds(0, 4), 0], out_sem.at[n])


def spread(queries, keys, values, grad_out):
    dma = pltpu.SemaphoreType.DMA
    return pl.pallas_call(
        spread_kernel,
        out_shape=jax.ShapeDtypeStruct((6, GROUPS, ROWS, WIDTH), jnp.bfloat16),
        in_specs=[pl.BlockSpec(memory_space=pl.ANY)] * 4,
        out_specs=pl.BlockSpec(memory_space=pl.ANY),
        scratch_shapes=[dma((15,)), dma((GROUPS,)), dma((GROUPS,)), dma((GROUPS,)), dma((GROUPS,))],
        compiler_params=pltpu.CompilerParams(collective_id=0, has_side_effects=True),
        name="spread",
    )(queries, keys, values, grad_out)


def dot_nt(a, b):
    return lax.dot_general(a, b, (((1,), (1,)), ((), ())), preferred_element_type=jnp.float32)


def dot_nn(a, b):
    return lax.dot_general(a, b, (((1,), (0,)), ((), ())), preferred_element_type=jnp.float32)


def dot_tn(a, b):
    return lax.dot_general(a, b, (((0,), (0,)), ((), ())), preferred_element_type=jnp.float32)


def attend_kernel(span_ref, level_ref, live_ref, held, bias_ref, o_out, dq_out, own_out, near_out,
                  data, table, score, total, own_b, near_b, o_b, dq_b, order, in_sem, out_sem):
    me, tile, y, x = place()
    my_head, active = head_of(y, x)
    inv_root = 1.0 / math.sqrt(WIDTH)

    @pl.when(active)
    def _():
        for g in range(GROUPS):
            order[span_ref[g]] = g
        fetches = []
        for p in range(GROUPS):
            fetch = pltpu.make_async_copy(
                held.at[:, order[p]], data.at[:, pl.ds(p * ROWS, ROWS)], in_sem.at[p])
            fetch.start()
            fetches.append(fetch)
        lane = lax.broadcasted_iota(jnp.int32, (1, HEADS), 1)
        for p in range(GROUPS):
            row = bias_ref[pl.ds(level_ref[p], 1), :]
            value = jnp.sum(jnp.where(lane == my_head, row, 0.0), axis=1, keepdims=True) * LOG2E
            table[p // 2, :, pl.ds((p % 2) * ROWS, ROWS)] = jnp.broadcast_to(value, (8, ROWS))
        total[...] = jnp.zeros_like(total)
        for fetch in fetches:
            fetch.wait()

        upper = lax.broadcasted_iota(jnp.int32, (PAIR, 1), 0) < ROWS
        right = lax.broadcasted_iota(jnp.int32, (1, PAIR), 1) >= ROWS

        @pl.loop(0, PAIRS)
        def _(i):
            rows = pl.ds(pl.multiple_of(i * PAIR, PAIR), PAIR)
            q = data[0, rows, :]
            g = data[1, rows, :]
            live_a = live_ref[order[2 * i] * TILES + tile]
            live_b = live_ref[order[2 * i + 1] * TILES + tile]

            def half(near):
                sides = 2 if near else 1
                live_row = jnp.where(upper, live_a, live_b) == 1
                row_mask = jnp.where(live_row, 0.0, NEG)

                def scores(j, side, diagonal):
                    cols = pl.ds(pl.multiple_of(j * PAIR, PAIR), PAIR)
                    s = dot_nt(q, data[2 + 2 * side, cols, :]) * (inv_root * LOG2E)
                    s = s + table[j, 0:1, :]
                    if side:
                        s = s + row_mask
                    if diagonal:
                        s = jnp.where(jnp.logical_and(upper, right), NEG, s)
                    score[side, j] = s
                    return jnp.maximum(s[:, :ROWS], s[:, ROWS:])

                def pass_a(j, peak):
                    for side in range(sides):
                        peak = jnp.maximum(peak, scores(j, side, False))
                    return peak

                peak = scores(i, 0, True)
                if near:
                    peak = jnp.maximum(peak, scores(i, 1, True))
                peak = lax.fori_loop(0, i, pass_a, peak)
                row_peak = jnp.max(peak, axis=1, keepdims=True)

                def pass_b(j, carry):
                    denom, acc = carry
                    cols = pl.ds(pl.multiple_of(j * PAIR, PAIR), PAIR)
                    for side in range(sides):
                        e = jnp.exp2(score[side, j] - row_peak)
                        score[side, j] = e
                        denom = denom + (e[:, :ROWS] + e[:, ROWS:])
                        acc = acc + dot_nn(e.astype(jnp.bfloat16), data[3 + 2 * side, cols, :])
                    return denom, acc

                zero = jnp.zeros((PAIR, WIDTH), jnp.float32)
                denom, acc = lax.fori_loop(0, i + 1, pass_b, (zero, zero))
                recip = 1.0 / jnp.sum(denom, axis=1, keepdims=True)
                attended = (acc * recip).astype(jnp.bfloat16)
                o_b[rows, :] = attended
                delta = jnp.sum(g.astype(jnp.float32) * attended.astype(jnp.float32),
                                axis=1, keepdims=True)

                def pass_c(j, dq):
                    cols = pl.ds(pl.multiple_of(j * PAIR, PAIR), PAIR)
                    for side in range(sides):
                        dp = dot_nt(g, data[3 + 2 * side, cols, :])
                        w = score[side, j] * recip
                        ds = (w * (dp - delta)).astype(jnp.bfloat16)
                        dq = dq + dot_nn(ds, data[2 + 2 * side, cols, :])
                        total[2 * side, cols, :] += dot_tn(ds, q)
                        total[2 * side + 1, cols, :] += dot_tn(w.astype(jnp.bfloat16), g)
                    return dq

                dq = lax.fori_loop(0, i + 1, pass_c, zero)
                dq_b[rows, :] = (dq * inv_root).astype(jnp.bfloat16)

            any_live = (live_a + live_b) > 0
            pl.when(any_live)(lambda: half(True))
            pl.when(jnp.logical_not(any_live))(lambda: half(False))

        own_b[0] = total[0] * inv_root
        own_b[1] = total[1]
        near_b[0] = (total[2] * inv_root).astype(jnp.bfloat16)
        near_b[1] = total[3].astype(jnp.bfloat16)
        copies = []
        for p in range(GROUPS):
            here = pl.ds(p * ROWS, ROWS)
            for n, (src, dst) in enumerate([
                (near_b.at[:, here], near_out.at[:, order[p]]),
                (own_b.at[:, here], own_out.at[:, order[p]]),
                (o_b.at[here], o_out.at[order[p]]),
                (dq_b.at[here], dq_out.at[order[p]]),
            ]):
                copy = pltpu.make_async_copy(src, dst, out_sem.at[n, p])
                copy.start()
                copies.append(copy)
        for copy in copies:
            copy.wait()


def attend(span_of_group, noise_level, next_live, held, level_bias):
    smem = pl.BlockSpec(memory_space=pltpu.SMEM)
    hbm = pl.BlockSpec(memory_space=pl.ANY)
    tokens = GROUPS * ROWS
    dma = pltpu.SemaphoreType.DMA
    return pl.pallas_call(
        attend_kernel,
        out_shape=(
            jax.ShapeDtypeStruct((GROUPS, ROWS, WIDTH), jnp.bfloat16),
            jax.ShapeDtypeStruct((GROUPS, ROWS, WIDTH), jnp.bfloat16),
            jax.ShapeDtypeStruct((2, GROUPS, ROWS, WIDTH), jnp.float32),
            jax.ShapeDtypeStruct((2, GROUPS, ROWS, WIDTH), jnp.bfloat16),
        ),
        in_specs=[smem, smem, smem, hbm, pl.BlockSpec(memory_space=pltpu.VMEM)],
        out_specs=(hbm, hbm, hbm, hbm),
        scratch_shapes=[
            pltpu.VMEM((6, tokens, WIDTH), jnp.bfloat16),
            pltpu.VMEM((PAIRS, 8, PAIR), jnp.float32),
            pltpu.VMEM((2, PAIRS, PAIR, PAIR), jnp.float32),
            pltpu.VMEM((4, tokens, WIDTH), jnp.float32),
            pltpu.VMEM((2, tokens, WIDTH), jnp.float32),
            pltpu.VMEM((2, tokens, WIDTH), jnp.bfloat16),
            pltpu.VMEM((tokens, WIDTH), jnp.bfloat16),
            pltpu.VMEM((tokens, WIDTH), jnp.bfloat16),
            pltpu.SMEM((GROUPS,), jnp.int32),
            dma((GROUPS,)),
            dma((4, GROUPS)),
        ],
        compiler_params=pltpu.CompilerParams(vmem_limit_bytes=48 * 1024 * 1024),
        name="attend",
    )(span_of_group, noise_level, next_live, held, level_bias)


def collect_kernel(o_ref, dq_ref, own_ref, near_ref, o_out, dq_out, dk_out, dv_out,
                   landed, ready, near_out, near_in, out_a, out_b, in_a, in_b):
    me, tile, y, x = place()
    before = lax.rem(tile + TILES - 1, TILES)
    after = lax.rem(tile + 1, TILES)
    my_head, active = head_of(y, x)
    meet(me, tile, y, x, before, after)
    mine = columns(my_head)

    def line(dy):
        return pl.ds(pl.multiple_of(lax.rem(y + dy, SIDE) * SIDE, SIDE), SIDE)

    @pl.when(active)
    def _():
        for dy in (2, 1, 3, 0):
            send(near_ref.at[:, line(dy)], landed.at[:, line(dy)], near_out.at[dy],
                 near_in.at[dy], (me, after))
        for n, (dy, dx) in enumerate(ORDER):
            other, _, _ = partner(y, x, dy, dx)
            send(o_ref.at[other], o_out.at[:, mine], out_a.at[n], in_a.at[me], (other, tile))
            send(dq_ref.at[other], dq_out.at[:, mine], out_a.at[n], in_a.at[me], (other, tile))
        pltpu.make_async_copy(o_ref.at[me], o_out.at[:, mine], in_a.at[me]).start()
        pltpu.make_async_copy(dq_ref.at[me], dq_out.at[:, mine], in_a.at[me]).start()
        for dy in (2, 1, 3, 0):
            await_bytes(landed.at[:, line(dy)], near_in.at[dy])
            ready[:, line(dy)] = (
                own_ref[:, line(dy)] + landed[:, line(dy)].astype(jnp.float32)
            ).astype(jnp.bfloat16)
            for dx in (2, 1, 3, 0):
                if (dy, dx) == (0, 0):
                    pltpu.make_async_copy(ready.at[0, me], dk_out.at[:, mine], in_b.at[me]).start()
                    pltpu.make_async_copy(ready.at[1, me], dv_out.at[:, mine], in_b.at[me]).start()
                    continue
                n = ORDER.index((dy, dx))
                other, _, _ = partner(y, x, dy, dx)
                send(ready.at[0, other], dk_out.at[:, mine], out_b.at[n], in_b.at[me], (other, tile))
                send(ready.at[1, other], dv_out.at[:, mine], out_b.at[n], in_b.at[me], (other, tile))

    for chip in range(GROUPS):
        if chip % SIDE != SIDE - 1 - chip // SIDE:
            await_bytes(ready.at[:, 0], in_a.at[chip])
            await_bytes(ready.at[:, 0], in_b.at[chip])

    @pl.when(active)
    def _():
        for n in range(len(ORDER)):
            await_bytes(ready.at[:, 0], out_a.at[n])
            await_bytes(ready.at[:, 0], out_b.at[n])
        for dy in range(SIDE):
            await_bytes(landed.at[:, line(dy)], near_out.at[dy])


def collect(attended, grad_queries, own, near):
    hbm = pl.BlockSpec(memory_space=pl.ANY)
    dma = pltpu.SemaphoreType.DMA
    result = jax.ShapeDtypeStruct((ROWS, HEADS * WIDTH), jnp.bfloat16)
    return pl.pallas_call(
        collect_kernel,
        out_shape=(result,) * 4,
        in_specs=[hbm, hbm, pl.BlockSpec(memory_space=pltpu.VMEM), hbm],
        out_specs=(hbm,) * 4,
        scratch_shapes=[
            pltpu.VMEM((2, GROUPS, ROWS, WIDTH), jnp.bfloat16),
            pltpu.VMEM((2, GROUPS, ROWS, WIDTH), jnp.bfloat16),
            dma((SIDE,)), dma((SIDE,)), dma((15,)), dma((15,)), dma((GROUPS,)), dma((GROUPS,)),
        ],
        compiler_params=pltpu.CompilerParams(collective_id=1, has_side_effects=True),
        name="collect",
    )(attended, grad_queries, own, near)


def per_device(queries, keys, values, grad_out, span_of_group, noise_level, next_live, level_bias):
    held = spread(queries, keys, values, grad_out)
    attended, grad_queries, own, near = attend(span_of_group, noise_level, next_live, held, level_bias)
    return collect(attended, grad_queries, own, near)


def solution(mesh):
    rows = P(("tm", "tile"), None)
    return jax.shard_map(
        per_device, mesh=mesh,
        in_specs=(rows, rows, rows, rows, P(), P(), P(), P()),
        out_specs=(rows, rows, rows, rows), check_vma=False,
    )
```

time: 685 us -> 134 us (0.20)
  the two profiles are of different devices: /device:TPU:0 before, /device:TPU:1 now
where the time goes in v1:
time: 134 us
  Pallas kernels  121 us (90%)
  local copies, waits for them, and re-layouts  12 us (9%)
    pallas_call x1, Pallas kernels, attend(): pl.pallas_call(attend_kernel, out_shape=(jax.ShapeDtypeStruct((GROUPS, RO...  55 us
    pallas_call x1, Pallas kernels, spread(): pl.pallas_call(spread_kernel, out_shape=jax.ShapeDtypeStruct((6, GROUPS,...  35.8 us
    pallas_call x1, Pallas kernels, collect(): pl.pallas_call(collect_kernel, out_shape=(result,) * 4, in_specs=[hbm, hb...  29.9 us
    unnamed x19, local copies, waits for them, and re-layouts  12 us

profile of v1, /device:TPU:1, one launch (start us, length us, event | category | flops | bytes accessed | tf_op | source)
XLA Modules:
  0.0 133.5 jit_solution(13370585046062714672)
XLA Ops:
  0.6 0.0 copy-start.6
  0.6 0.0 copy-start.5
  0.7 0.0 copy-start.4
  0.7 1.1 copy.12.bias_ref
  1.7 35.8 %spread.1.held = bf16[6,16,128,128]{3,2,1,0:T(8,128)(2,1)} custom-call(bf16[128,1536]{1,0:T(8,128)(2,1)} %q_ref.1, bf16[128,1536]{1,0:T(8,128)(2,1)} %k_ref.1, bf16[128,1536]{1,0:T(8,128)(2,1)} %v_ref.1, bf16[128,1536]{1,0:T(8,128)(2,1)} %g_ref.1), custom_call_target="tpu_custom_call" | custom-call | tf_op jit(solution)/shard_map/spread/pallas_call | solution.py:119
  37.6 0.0 copy-done.6
  37.6 0.0 copy-done.5
  37.6 0.0 copy-done.4
  37.6 55.0 %attend.1 = (bf16[16,128,128]{2,1,0:T(8,128)(2,1)S(1)}, bf16[16,128,128]{2,1,0:T(8,128)(2,1)S(1)}, f32[2,16,128,128]{3,2,1,0:T(8,128)S(1)}, bf16[2,16,128,128]{3,2,1,0:T(8,128)(2,1)S(1)}) custom-call(s32[16]{0:T(128)S(1)} %copy-done.4, s32[16]{0:T(128)S(1)} %copy-done.5, s32[128]{0:T(128)S(1)} %copy-done.6, bf16[6,16,128,128]{3,2,1,0:T(8,128)(2,1)} %spread.1.held, ...), custom_call_target="tpu_custom_call" | custom-call | tf_op jit(solution)/shard_map/attend/pallas_call | solution.py:266
  92.6 0.0 copy-start
  92.6 1.3 copy-done
  93.9 0.0 copy-start.1
  93.9 1.0 copy-done.1
  94.9 0.0 copy-start.2
  94.9 0.8 copy-done.2
  95.7 0.0 copy-start.3
  95.7 0.8 copy-done.3
  96.5 29.9 %collect.1 = (bf16[128,1536]{1,0:T(8,128)(2,1)}, bf16[128,1536]{1,0:T(8,128)(2,1)}, bf16[128,1536]{1,0:T(8,128)(2,1)}, bf16[128,1536]{1,0:T(8,128)(2,1)}) custom-call(bf16[16,128,128]{2,1,0:T(8,128)(2,1)} %copy-done.2, bf16[16,128,128]{2,1,0:T(8,128)(2,1)} %copy-done.3, f32[2,16,128,128]{3,2,1,0:T(8,128)} %copy-done, bf16[2,16,128,128]{3,2,1,0:T(8,128)(2,1)} %copy-done.1), custom_call_target="tpu_custom_call" | custom-call | tf_op jit(solution)/shard_map/collect/pallas_call | solution.py:350
  126.5 1.8 %copy.17 = bf16[128,1536]{1,0:T(8,128)(2,1)} copy(bf16[128,1536]{1,0:T(8,128)(2,1)} %get-tuple-element.16) | data formatting | bytes 786432
  128.2 1.8 %copy.18 = bf16[128,1536]{1,0:T(8,128)(2,1)} copy(bf16[128,1536]{1,0:T(8,128)(2,1)} %get-tuple-element.17) | data formatting | bytes 786432
  130.0 1.8 %copy.19 = bf16[128,1536]{1,0:T(8,128)(2,1)} copy(bf16[128,1536]{1,0:T(8,128)(2,1)} %get-tuple-element.18) | data formatting | bytes 786432
  131.8 1.8 %copy.20 = bf16[128,1536]{1,0:T(8,128)(2,1)} copy(bf16[128,1536]{1,0:T(8,128)(2,1)} %get-tuple-element.19) | data formatting | bytes 786432
Async XLA Ops:
  0.6 36.9 %copy-start.6 = (s32[128]{0:T(128)S(1)}, s32[128]{0:T(128)}, u32[]{:S(2)}) copy-start(s32[128]{0:T(128)} %live_ref.1) | copy-start | bytes 1540
  0.6 36.9 %copy-start.5 = (s32[16]{0:T(128)S(1)}, s32[16]{0:T(128)}, u32[]{:S(2)}) copy-start(s32[16]{0:T(128)} %level_ref.1) | copy-start | bytes 196
  0.7 36.9 %copy-start.4 = (s32[16]{0:T(128)S(1)}, s32[16]{0:T(128)}, u32[]{:S(2)}) copy-start(s32[16]{0:T(128)} %span_ref.1) | copy-start | bytes 196
  92.6 1.3 %copy-start = (f32[2,16,128,128]{3,2,1,0:T(8,128)}, f32[2,16,128,128]{3,2,1,0:T(8,128)S(1)}, u32[]{:S(2)}) copy-start(f32[2,16,128,128]{3,2,1,0:T(8,128)S(1)} %get-tuple-element.10.own_ref) | copy-start | bytes 6291460
  93.9 1.0 copy-start.1
  94.9 0.8 copy-start.2
  95.7 0.8 copy-start.3
